TPU v7x, 256 devices: a whole 4x4x8 slice. The times are simulated.
256 devices in a mesh: gx: 32 (over y, z), gy: 8 (over x, core).
Axes of the slice: x: 4, y: 4, z: 8, core: 2. Of those that a mesh axis runs over, the one named last changes fastest.
Arguments:
- densities: bfloat16 [24576, 32, 128], P(('gx', 'gy')), may hold values from -6 to 6
- geometry: float32 [24576, 7, 128], P(('gx', 'gy')), as said below
- near_ids: int32 [24576, 8], P(('gx', 'gy')), may hold values from 0 to 24575, as said below
- basis_in: bfloat16 [24576, 64, 128], P(('gx', 'gy')), may hold values from -0.5 to 0.5
- basis_out: bfloat16 [24576, 64, 128], P(('gx', 'gy')), may hold values from -0.75 to 0.75
- leaf_up: bfloat16 [24576, 64, 64], P(('gx', 'gy')), may hold values from -0.078125 to 0.078125
- leaf_down: bfloat16 [24576, 64, 64], P(('gx', 'gy')), may hold values from -0.75 to 0.75
- leaf_coupling: bfloat16 [24576, 6, 64, 64], P(('gx', 'gy')), may hold values from -0.3125 to 0.3125
- leaf_far: int32 [24576, 6], P(('gx', 'gy')), may hold values from 0 to 24575, as said below
- leaf_count: int32 [24576], P(('gx', 'gy')), may hold values from 1 to 6, as said below
- cluster_up: bfloat16 [256, 64, 64], P(('gx', 'gy')), may hold values from -0.25 to 0.25
- cluster_down: bfloat16 [256, 64, 64], P(('gx', 'gy')), may hold values from -0.75 to 0.75
- cluster_coupling: bfloat16 [256, 6, 64, 64], P(('gx', 'gy')), may hold values from -0.3125 to 0.3125
- cluster_far: int32 [256, 6], P(('gx', 'gy')), may hold values from 0 to 255, as said below
- group_up: bfloat16 [32, 64, 64], replicated, may hold values from -0.375 to 0.375
- group_down: bfloat16 [32, 64, 64], P('gx'), may hold values from -0.75 to 0.75
- group_coupling: bfloat16 [32, 6, 64, 64], P('gx'), may hold values from -0.3125 to 0.3125
- group_far: int32 [32, 6], P('gx'), may hold values from 0 to 31, as said below
- root_coupling: bfloat16 [8, 8, 64, 64], replicated, may hold values from -0.25 to 0.25
Outputs:
- potential: float32 [24576, 32, 128], P(('gx', 'gy'))
Inputs may be any that keep to these rules, and one draw needn't show every extreme that they name: `near_ids`: row l names 8 different leaves of a window of 9 consecutive leaves that contains l, centred on l where the ends allow. `leaf_far`: row l names 6 different leaves held by l's device or its two neighbours in leaf order, none within 4 leaves of l; only the first leaf_count[l] entries are used. `leaf_count`: every device holds a leaf with 6. `cluster_far`: row u names 6 different level-two clusters other than u, of u's group or the two groups beside it. `group_far`: row g names 6 different level-one clusters other than g. `geometry`: rows 0 to 2 hold a panel's centre, rows 3 to 5 its unit normal, row 6 its area, from 0.25 to 2.
All inputs are finite; a program needn't handle non-finite values.
Results may differ from a plain program's by a relative error of at most 0.012.
Values may be sent and summed in bfloat16 or wider, within the bound.
A program may use at most 128 MiB of HBM per device.

v0:
```python
import math
import jax
import jax.numpy as jnp
from jax import lax
from jax.sharding import PartitionSpec as P

REACH = 4
BRANCH = 4
four_pi = 4.0 * math.pi
leaf_block = 8


def padded(cells, sides, width):
    for axis, dim in sides:
        count = lax.axis_size(axis)
        ends = count - 1
        head = lax.slice_in_dim(cells, 0, width, axis=dim)
        tail = lax.slice_in_dim(cells, cells.shape[dim] - width, cells.shape[dim], axis=dim)
        cells = jnp.concatenate(
            [
                lax.ppermute(tail, axis, [(i, (i + 1) % count) for i in range(ends)]),
                cells,
                lax.ppermute(head, axis, [((i + 1) % count, i) for i in range(ends)]),
            ],
            axis=dim,
        )
    return cells


def near_kernel(target, source):
    offsets = [
        target[:, coord_id, :, None, None] - source[:, None, :, coord_id, :]
        for coord_id in range(3)
    ]
    distance = offsets[0] * offsets[0] + offsets[1] * offsets[1] + offsets[2] * offsets[2]
    facing = (
        source[:, None, :, 3, :] * offsets[0]
        + source[:, None, :, 4, :] * offsets[1]
        + source[:, None, :, 5, :] * offsets[2]
    )
    panel_area = source[:, None, :, 6, :]
    spread = distance + panel_area
    return panel_area * facing / (four_pi * spread * jnp.sqrt(spread))


def on_device(
    densities,
    geometry,
    near_ids,
    basis_in,
    basis_out,
    leaf_up,
    leaf_down,
    leaf_coupling,
    leaf_far,
    leaf_count,
    cluster_up,
    cluster_down,
    cluster_coupling,
    cluster_far,
    group_up,
    group_down,
    group_coupling,
    group_far,
    root_coupling,
):
    wide = jnp.float32
    narrow = jnp.bfloat16
    leaves = densities.shape[0]
    coeff_order = basis_in.shape[1]
    columns = densities.shape[1]
    flat = coeff_order * columns
    first_leaf = lax.axis_index(("gx", "gy")) * leaves
    gx_index = lax.axis_index("gx")
    group_size = lax.axis_size("gy")
    groups = lax.axis_size("gx")
    leaf_coeffs = jnp.einsum(
        "lkm,lrm->lkr", basis_in, densities, preferred_element_type=wide
    ).astype(narrow)
    mid_coeffs = jnp.einsum(
        "lik,lkr->ir", leaf_up, leaf_coeffs, preferred_element_type=wide
    ).astype(narrow)
    mid_term = jnp.dot(cluster_up[0], mid_coeffs, preferred_element_type=wide).reshape(1, flat)
    mid_flat = mid_coeffs.reshape(1, flat)
    siblings = lax.all_gather(mid_flat, "gy", axis=0, tiled=True)
    group_sum = lax.psum(mid_term, "gy")
    nearby = padded(siblings, (("gx", 0),), group_size)
    mid_picked = jnp.take(nearby, cluster_far[0] - (gx_index - 1) * group_size, axis=0)
    top_coeffs = lax.all_gather(group_sum.astype(narrow), "gx", axis=0, tiled=True)
    top_block = top_coeffs.reshape(groups, coeff_order, columns)
    root_terms = jnp.einsum("gik,gkr->gir", group_up, top_block, preferred_element_type=wide)
    root_coeffs = jnp.sum(
        root_terms.reshape(groups // BRANCH, BRANCH, coeff_order, columns), axis=1
    ).astype(narrow)
    root_row = lax.dynamic_index_in_dim(root_coupling, gx_index // BRANCH, 0, keepdims=False)
    root_field = jnp.einsum(
        "sik,skr->ir", root_row, root_coeffs, preferred_element_type=wide
    ).astype(narrow)
    top_picked = jnp.take(top_block, group_far[0], axis=0)
    top_field = (
        jnp.einsum("fik,fkr->ir", group_coupling[0], top_picked, preferred_element_type=wide)
        + jnp.dot(group_down[0], root_field, preferred_element_type=wide)
    ).astype(narrow)
    mid_block = mid_picked.reshape(-1, coeff_order, columns)
    mid_field = (
        jnp.einsum("fik,fkr->ir", cluster_coupling[0], mid_block, preferred_element_type=wide)
        + jnp.dot(cluster_down[0], top_field, preferred_element_type=wide)
    ).astype(narrow)
    coeff_rim = padded(leaf_coeffs.reshape(leaves, flat), ((("gx", "gy"), 0),), leaves)
    picked = jnp.take(coeff_rim, leaf_far - (first_leaf - leaves), axis=0).reshape(
        leaves, -1, coeff_order, columns
    )
    live_mask = (lax.broadcasted_iota(jnp.int32, leaf_far.shape, 1) < leaf_count[:, None]).astype(
        narrow
    )
    picked = picked * live_mask[:, :, None, None]
    leaf_field = (
        jnp.einsum("lfik,lfkr->lir", leaf_coupling, picked, preferred_element_type=wide)
        + jnp.einsum("lik,kr->lir", leaf_down, mid_field, preferred_element_type=wide)
    ).astype(narrow)
    far_part = jnp.einsum("lkr,lkm->lrm", leaf_field, basis_out, preferred_element_type=wide)
    values_rim = padded(densities, ((("gx", "gy"), 0),), REACH)
    shape_rim = padded(geometry, ((("gx", "gy"), 0),), REACH)
    near_local = near_ids - (first_leaf - REACH)

    def near_block(pieces):
        target, indices = pieces
        source = jnp.take(shape_rim, indices, axis=0)
        values = jnp.take(values_rim, indices, axis=0)
        kernel = near_kernel(target, source).astype(narrow)
        return jnp.einsum("bmnj,bnrj->brm", kernel, values, preferred_element_type=wide)

    near_part = lax.map(
        near_block,
        (
            geometry.reshape(leaves // leaf_block, leaf_block, 7, -1),
            near_local.reshape(leaves // leaf_block, leaf_block, -1),
        ),
    )
    return far_part + near_part.reshape(far_part.shape)


def solution(mesh):
    return jax.shard_map(
        on_device,
        mesh=mesh,
        in_specs=(
            P(("gx", "gy"), None, None),
            P(("gx", "gy"), None, None),
            P(("gx", "gy"), None),
            P(("gx", "gy"), None, None),
            P(("gx", "gy"), None, None),
            P(("gx", "gy"), None, None),
            P(("gx", "gy"), None, None),
            P(("gx", "gy"), None, None, None),
            P(("gx", "gy"), None),
            P(("gx", "gy")),
            P(("gx", "gy"), None, None),
            P(("gx", "gy"), None, None),
            P(("gx", "gy"), None, None, None),
            P(("gx", "gy"), None),
            P(),
            P("gx", None, None),
            P("gx", None, None, None),
            P("gx", None),
            P(),
        ),
        out_specs=P(("gx", "gy"), None, None),
        check_vma=False,
    )
```

profile of v0, /device:TPU:8, one launch (start us, length us, event | category | flops | bytes accessed | tf_op | source)
XLA Modules:
  0.0 328.0 jit_solution(2928487035204301218)
XLA Ops:
  4.9 9.3 %collective-permute-start.1 = (bf16[96,2048]{1,0:T(8,128)(2,1)}, bf16[96,2048]{1,0:T(8,128)(2,1)}, u32[]{:S(2)}, u32[]{:S(2)}) collective-permute-start(bf16[96,2048]{1,0:T(8,128)(2,1)} %copy.66), channel_id=1, source_target_pairs={{1,0},{2,1},{3,2},{4,3},{5,4},{6,5},{7,6},{8,7},{9,8},{10,9},{11,1... | collective-permute-start | bytes 1179656 | tf_op jit(solution)/shard_map/ppermute | solution.py:23
  19.3 8.0 %collective-permute-start.7 = (f32[4,7,128]{2,1,0:T(8,128)S(1)}, f32[4,7,128]{2,1,0:T(8,128)S(1)}, u32[]{:S(2)}, u32[]{:S(2)}) collective-permute-start(f32[4,7,128]{2,1,0:T(8,128)S(1)} %get-tuple-element.83), channel_id=1, source_target_pairs={{1,0},{2,1},{3,2},{4,3},{5,4},{6,5},{7,6},{8,7},{9,8},{10,9},{11,1... | collective-permute-start | bytes 43016 | tf_op jit(solution)/shard_map/ppermute | solution.py:23
  27.3 4.0 %copy.72 = bf16[96,64,64]{2,1,0:T(8,128)(2,1)} copy(bf16[96,64,64]{0,2,1:T(8,128)(2,1)} %param.26) | data formatting | bytes 1572864 | tf_op args[5]
  33.5 12.8 %all-gather = bf16[8,1,2048]{2,1,0:T(2,128)(2,1)S(1)} all-gather(bf16[1,1,2048]{2,1,0:T(2,128)(2,1)S(1)} %reshape.240), channel_id=1, replica_groups=mesh['gx'=32,'gy'=8] {'gy'}, dimensions={0}, use_global_device_ids=true | all-gather | bytes 36864 | tf_op jit(solution)/shard_map/all_gather | solution.py:85
  50.4 24.5 %psum.7 = bf16[1,2048]{1,0:T(2,128)(2,1)S(1)} all-reduce(f32[1,2048]{1,0:T(1,128)S(1)} %reshape.189), channel_id=1, replica_groups=mesh['gx'=32,'gy'=8] {'gy'}, use_global_device_ids=true, to_apply=%region_0.0 | all-reduce | flops 2048 | bytes 12288 | tf_op jit(solution)/shard_map/psum | solution.py:86
  74.9 48.0 %all-gather.1 = bf16[32,1,2048]{2,1,0:T(2,128)(2,1)S(1)} all-gather(bf16[1,1,2048]{2,1,0:T(2,128)(2,1)S(1)} %bitcast.169), channel_id=1, replica_groups=mesh['gx'=32,'gy'=8] {'gx'}, dimensions={0}, use_global_device_ids=true | all-gather | bytes 135168 | tf_op jit(solution)/shard_map/all_gather | solution.py:89
  133.4 16.1 %copy.71 = bf16[96,6,64,64]{3,2,1,0:T(8,128)(2,1)} copy(bf16[96,6,64,64]{0,3,2,1:T(8,128)(2,1)} %param.28) | data formatting | bytes 9437184 | tf_op args[7]
  154.0 8.0 %collective-permute-start.5 = (bf16[4,32,128]{2,1,0:T(8,128)(2,1)S(1)}, bf16[4,32,128]{2,1,0:T(8,128)(2,1)S(1)}, u32[]{:S(2)}, u32[]{:S(2)}) collective-permute-start(bf16[4,32,128]{2,1,0:T(8,128)(2,1)S(1)} %get-tuple-element.81), channel_id=1, source_target_pairs={{1,0},{2,1},{3,2},{4,3},{5,4},{6,5},{7,6},{8,7},{9,8},{10,9},{11,1... | collective-permute-start | bytes 98312 | tf_op jit(solution)/shard_map/ppermute | solution.py:23
  164.7 130.7 %while.10 = (s32[]{:T(128)}, f32[12,8,32,128]{3,2,1,0:T(8,128)}, s32[12,8,8]{2,1,0:T(8,128)}, bf16[104,32,128]{2,1,0:T(8,128)(2,1)S(1)}, f32[104,7,128]{2,1,0:T(...) while((s32[]{:T(128)}, f32[12,8,32,128]{3,2,1,0:T(8,128)}, s32[12,8,8]{2,1,0:T(8,128)}, ...), condition=%wide.region_3.4_spmd, body=%wide.region_2.3_spmd.sunk | while | flops 87352896 | bytes 3410213 | solution.py:133
  169.7 5.9 %fusion.84 = f32[12,8,32,128]{3,2,1,0:T(8,128)} fusion(f32[12,8,32,128]{3,2,1,0:T(8,128)} %get-tuple-element.149, s32[]{:T(128)S(6)} %copy.97, f32[8,8,128]{2,1,0:T(8,128)S(1)} %bitcast.159, f32[8,128]{1,0:T(8,128)} %get-tuple-element.132, f32[8,8,128]{2,1,0:T(8,128)S(1)} %bitcast.160, f32[8,8,128]{2,1,0:T(8,128)S(1)} %bitcast.161, ...), kind=kOutput, calls=%fused_computation.21.clone.1 | convolution fusion | flops 87293952 | bytes 897092 | tf_op jit(solution)/shard_map/while/body/eval_jaxpr/bmnj,bnrj->brm/dot_general | solution.py:131
  180.6 5.9 %fusion.84 = f32[12,8,32,128]{3,2,1,0:T(8,128)} fusion(f32[12,8,32,128]{3,2,1,0:T(8,128)} %get-tuple-element.149, s32[]{:T(128)S(6)} %copy.97, f32[8,8,128]{2,1,0:T(8,128)S(1)} %bitcast.159, f32[8,128]{1,0:T(8,128)} %get-tuple-element.132, f32[8,8,128]{2,1,0:T(8,128)S(1)} %bitcast.160, f32[8,8,128]{2,1,0:T(8,128)S(1)} %bitcast.161, ...), kind=kOutput, calls=%fused_computation.21.clone.1 | convolution fusion | flops 87293952 | bytes 897092 | tf_op jit(solution)/shard_map/while/body/eval_jaxpr/bmnj,bnrj->brm/dot_general | solution.py:131
  191.5 5.9 %fusion.84 = f32[12,8,32,128]{3,2,1,0:T(8,128)} fusion(f32[12,8,32,128]{3,2,1,0:T(8,128)} %get-tuple-element.149, s32[]{:T(128)S(6)} %copy.97, f32[8,8,128]{2,1,0:T(8,128)S(1)} %bitcast.159, f32[8,128]{1,0:T(8,128)} %get-tuple-element.132, f32[8,8,128]{2,1,0:T(8,128)S(1)} %bitcast.160, f32[8,8,128]{2,1,0:T(8,128)S(1)} %bitcast.161, ...), kind=kOutput, calls=%fused_computation.21.clone.1 | convolution fusion | flops 87293952 | bytes 897092 | tf_op jit(solution)/shard_map/while/body/eval_jaxpr/bmnj,bnrj->brm/dot_general | solution.py:131
  202.4 5.9 %fusion.84 = f32[12,8,32,128]{3,2,1,0:T(8,128)} fusion(f32[12,8,32,128]{3,2,1,0:T(8,128)} %get-tuple-element.149, s32[]{:T(128)S(6)} %copy.97, f32[8,8,128]{2,1,0:T(8,128)S(1)} %bitcast.159, f32[8,128]{1,0:T(8,128)} %get-tuple-element.132, f32[8,8,128]{2,1,0:T(8,128)S(1)} %bitcast.160, f32[8,8,128]{2,1,0:T(8,128)S(1)} %bitcast.161, ...), kind=kOutput, calls=%fused_computation.21.clone.1 | convolution fusion | flops 87293952 | bytes 897092 | tf_op jit(solution)/shard_map/while/body/eval_jaxpr/bmnj,bnrj->brm/dot_general | solution.py:131
  213.3 5.9 %fusion.84 = f32[12,8,32,128]{3,2,1,0:T(8,128)} fusion(f32[12,8,32,128]{3,2,1,0:T(8,128)} %get-tuple-element.149, s32[]{:T(128)S(6)} %copy.97, f32[8,8,128]{2,1,0:T(8,128)S(1)} %bitcast.159, f32[8,128]{1,0:T(8,128)} %get-tuple-element.132, f32[8,8,128]{2,1,0:T(8,128)S(1)} %bitcast.160, f32[8,8,128]{2,1,0:T(8,128)S(1)} %bitcast.161, ...), kind=kOutput, calls=%fused_computation.21.clone.1 | convolution fusion | flops 87293952 | bytes 897092 | tf_op jit(solution)/shard_map/while/body/eval_jaxpr/bmnj,bnrj->brm/dot_general | solution.py:131
  224.2 5.9 %fusion.84 = f32[12,8,32,128]{3,2,1,0:T(8,128)} fusion(f32[12,8,32,128]{3,2,1,0:T(8,128)} %get-tuple-element.149, s32[]{:T(128)S(6)} %copy.97, f32[8,8,128]{2,1,0:T(8,128)S(1)} %bitcast.159, f32[8,128]{1,0:T(8,128)} %get-tuple-element.132, f32[8,8,128]{2,1,0:T(8,128)S(1)} %bitcast.160, f32[8,8,128]{2,1,0:T(8,128)S(1)} %bitcast.161, ...), kind=kOutput, calls=%fused_computation.21.clone.1 | convolution fusion | flops 87293952 | bytes 897092 | tf_op jit(solution)/shard_map/while/body/eval_jaxpr/bmnj,bnrj->brm/dot_general | solution.py:131
  235.1 5.9 %fusion.84 = f32[12,8,32,128]{3,2,1,0:T(8,128)} fusion(f32[12,8,32,128]{3,2,1,0:T(8,128)} %get-tuple-element.149, s32[]{:T(128)S(6)} %copy.97, f32[8,8,128]{2,1,0:T(8,128)S(1)} %bitcast.159, f32[8,128]{1,0:T(8,128)} %get-tuple-element.132, f32[8,8,128]{2,1,0:T(8,128)S(1)} %bitcast.160, f32[8,8,128]{2,1,0:T(8,128)S(1)} %bitcast.161, ...), kind=kOutput, calls=%fused_computation.21.clone.1 | convolution fusion | flops 87293952 | bytes 897092 | tf_op jit(solution)/shard_map/while/body/eval_jaxpr/bmnj,bnrj->brm/dot_general | solution.py:131
  246.0 5.9 %fusion.84 = f32[12,8,32,128]{3,2,1,0:T(8,128)} fusion(f32[12,8,32,128]{3,2,1,0:T(8,128)} %get-tuple-element.149, s32[]{:T(128)S(6)} %copy.97, f32[8,8,128]{2,1,0:T(8,128)S(1)} %bitcast.159, f32[8,128]{1,0:T(8,128)} %get-tuple-element.132, f32[8,8,128]{2,1,0:T(8,128)S(1)} %bitcast.160, f32[8,8,128]{2,1,0:T(8,128)S(1)} %bitcast.161, ...), kind=kOutput, calls=%fused_computation.21.clone.1 | convolution fusion | flops 87293952 | bytes 897092 | tf_op jit(solution)/shard_map/while/body/eval_jaxpr/bmnj,bnrj->brm/dot_general | solution.py:131
  256.9 5.9 %fusion.84 = f32[12,8,32,128]{3,2,1,0:T(8,128)} fusion(f32[12,8,32,128]{3,2,1,0:T(8,128)} %get-tuple-element.149, s32[]{:T(128)S(6)} %copy.97, f32[8,8,128]{2,1,0:T(8,128)S(1)} %bitcast.159, f32[8,128]{1,0:T(8,128)} %get-tuple-element.132, f32[8,8,128]{2,1,0:T(8,128)S(1)} %bitcast.160, f32[8,8,128]{2,1,0:T(8,128)S(1)} %bitcast.161, ...), kind=kOutput, calls=%fused_computation.21.clone.1 | convolution fusion | flops 87293952 | bytes 897092 | tf_op jit(solution)/shard_map/while/body/eval_jaxpr/bmnj,bnrj->brm/dot_general | solution.py:131
  267.8 5.9 %fusion.84 = f32[12,8,32,128]{3,2,1,0:T(8,128)} fusion(f32[12,8,32,128]{3,2,1,0:T(8,128)} %get-tuple-element.149, s32[]{:T(128)S(6)} %copy.97, f32[8,8,128]{2,1,0:T(8,128)S(1)} %bitcast.159, f32[8,128]{1,0:T(8,128)} %get-tuple-element.132, f32[8,8,128]{2,1,0:T(8,128)S(1)} %bitcast.160, f32[8,8,128]{2,1,0:T(8,128)S(1)} %bitcast.161, ...), kind=kOutput, calls=%fused_computation.21.clone.1 | convolution fusion | flops 87293952 | bytes 897092 | tf_op jit(solution)/shard_map/while/body/eval_jaxpr/bmnj,bnrj->brm/dot_general | solution.py:131
  278.7 5.9 %fusion.84 = f32[12,8,32,128]{3,2,1,0:T(8,128)} fusion(f32[12,8,32,128]{3,2,1,0:T(8,128)} %get-tuple-element.149, s32[]{:T(128)S(6)} %copy.97, f32[8,8,128]{2,1,0:T(8,128)S(1)} %bitcast.159, f32[8,128]{1,0:T(8,128)} %get-tuple-element.132, f32[8,8,128]{2,1,0:T(8,128)S(1)} %bitcast.160, f32[8,8,128]{2,1,0:T(8,128)S(1)} %bitcast.161, ...), kind=kOutput, calls=%fused_computation.21.clone.1 | convolution fusion | flops 87293952 | bytes 897092 | tf_op jit(solution)/shard_map/while/body/eval_jaxpr/bmnj,bnrj->brm/dot_general | solution.py:131
  289.6 5.9 %fusion.84 = f32[12,8,32,128]{3,2,1,0:T(8,128)} fusion(f32[12,8,32,128]{3,2,1,0:T(8,128)} %get-tuple-element.149, s32[]{:T(128)S(6)} %copy.97, f32[8,8,128]{2,1,0:T(8,128)S(1)} %bitcast.159, f32[8,128]{1,0:T(8,128)} %get-tuple-element.132, f32[8,8,128]{2,1,0:T(8,128)S(1)} %bitcast.160, f32[8,8,128]{2,1,0:T(8,128)S(1)} %bitcast.161, ...), kind=kOutput, calls=%fused_computation.21.clone.1 | convolution fusion | flops 87293952 | bytes 897092 | tf_op jit(solution)/shard_map/while/body/eval_jaxpr/bmnj,bnrj->brm/dot_general | solution.py:131
  296.5 4.3 %fusion.37 = f32[32,96,64]{2,0,1:T(8,128)} fusion(bf16[96,64,64]{2,1,0:T(8,128)(2,1)} %copy.78, f32[32,64]{1,0:T(8,128)S(1)} %convolution_bitcast_fusion.3, bf16[32,64]{1,0:T(8,128)(2,1)} %fusion.33, bf16[1,64,64]{2,1,0:T(8,128)(2,1)} %param.32), kind=kOutput, calls=%fused_computation.60 | convolution fusion | flops 25432064 | bytes 1593344 | tf_op jit(solution)/shard_map/lik,kr->lir/dot_general | solution.py:119
  306.1 11.7 %gather.23 = bf16[96,6,64,32]{3,2,1,0:T(8,128)(2,1)} reshape(bf16[576,2048]{1,0:T(8,128)(2,1)} %gather_fusion.2) | data formatting | bytes 4718592 | tf_op jit(solution)/shard_map/jit(_take)/gather | solution.py:110
  317.8 10.3 %bitcast_add_fusion.1 = f32[96,32,128]{2,1,0:T(8,128)} fusion(f32[12,8,32,128]{3,2,1,0:T(8,128)} %get-tuple-element.37, bf16[96,64,128]{2,1,0:T(8,128)(2,1)S(1)} %copy-done, f32[32,96,64]{2,0,1:T(8,128)S(1)} %copy-done.1, bf16[96,6,64,64]{3,2,1,0:T(8,128)(2,1)} %copy.71, bf16[96,6,64,32]{3,2,1,0:T(8,128)(2,1)} %gather.23, pred[96,6]{1,0:T(8,128)(4,1)S(1)} %copy-done.6, ...), kind=kOutput, calls=%fused_computation.44 | convolution fusion | flops 204472320 | bytes 12584640 | tf_op jit(solution)/shard_map/lkr,lkm->lrm/dot_general | solution.py:121
  (201 shorter events, 100.0 us)
Async XLA Ops:
  0.0 317.8 %copy-start = (bf16[96,64,128]{2,1,0:T(8,128)(2,1)S(1)}, bf16[96,64,128]{2,1,0:T(8,128)(2,1)}, u32[]{:S(2)}) copy-start(bf16[96,64,128]{2,1,0:T(8,128)(2,1)} %param.25) | copy-start | bytes 4718596
  4.9 295.9 %collective-permute-start.1 = (bf16[96,2048]{1,0:T(8,128)(2,1)}, bf16[96,2048]{1,0:T(8,128)(2,1)}, u32[]{:S(2)}, u32[]{:S(2)}) collective-permute-start(bf16[96,2048]{1,0:T(8,128)(2,1)} %copy.66), channel_id=1, source_target_pairs={{1,0},{2,1},{3,2},{4,3},{5,4},{6,5},{7,6},{8,7},{9,8},{10,9},{11,1... | collective-permute-start | bytes 1179656 | tf_op jit(solution)/shard_map/ppermute | solution.py:23
  14.2 286.6 %collective-permute-start = (bf16[96,2048]{1,0:T(8,128)(2,1)}, bf16[96,2048]{1,0:T(8,128)(2,1)}, u32[]{:S(2)}, u32[]{:S(2)}) collective-permute-start(bf16[96,2048]{1,0:T(8,128)(2,1)} %copy.66), channel_id=1, source_target_pairs={{0,1},{1,2},{2,3},{3,4},{4,5},{5,6},{6,7},{7,8},{8,9},{9,10},{10,1... | collective-permute-start | bytes 1179656 | tf_op jit(solution)/shard_map/ppermute | solution.py:21
  17.4 132.2 %collective-permute-start.6 = (f32[4,7,128]{2,1,0:T(8,128)S(1)}, f32[4,7,128]{2,1,0:T(8,128)S(1)}, u32[]{:S(2)}, u32[]{:S(2)}) collective-permute-start(f32[4,7,128]{2,1,0:T(8,128)S(1)} %get-tuple-element.82), channel_id=1, source_target_pairs={{0,1},{1,2},{2,3},{3,4},{4,5},{5,6},{6,7},{7,8},{8,9},{9,10},{10,1... | collective-permute-start | bytes 43016 | tf_op jit(solution)/shard_map/ppermute | solution.py:21
  19.3 29.0 %copy-start.10 = (s32[1,6]{1,0:T(1,128)S(1)}, s32[1,6]{1,0:T(1,128)}, u32[]{:S(2)}) copy-start(s32[1,6]{1,0:T(1,128)} %param.34) | copy-start | bytes 76
  19.3 29.0 %copy-start.11 = (s32[1,6]{1,0:T(1,128)S(1)}, s32[1,6]{1,0:T(1,128)}, u32[]{:S(2)}) copy-start(s32[1,6]{1,0:T(1,128)} %param.38) | copy-start | bytes 76
  19.3 29.8 %copy-start.9 = (s32[96]{0:T(128)S(1)}, s32[96]{0:T(128)}, u32[]{:S(2)}) copy-start(s32[96]{0:T(128)} %param.30) | copy-start | bytes 1156
  19.3 30.5 %copy-start.7 = (s32[96,6]{0,1:T(8,128)S(1)}, s32[96,6]{0,1:T(8,128)}, u32[]{:S(2)}) copy-start(s32[96,6]{0,1:T(8,128)} %param.29) | copy-start | bytes 6916
  19.3 30.8 %copy-start.4 = (bf16[1,64,64]{2,1,0:T(8,128)(2,1)S(1)}, bf16[1,64,64]{2,1,0:T(8,128)(2,1)}, u32[]{:S(2)}) copy-start(bf16[1,64,64]{2,1,0:T(8,128)(2,1)} %param.31) | copy-start | bytes 24580
  19.3 132.6 %collective-permute-start.7 = (f32[4,7,128]{2,1,0:T(8,128)S(1)}, f32[4,7,128]{2,1,0:T(8,128)S(1)}, u32[]{:S(2)}, u32[]{:S(2)}) collective-permute-start(f32[4,7,128]{2,1,0:T(8,128)S(1)} %get-tuple-element.83), channel_id=1, source_target_pairs={{1,0},{2,1},{3,2},{4,3},{5,4},{6,5},{7,6},{8,7},{9,8},{10,9},{11,1... | collective-permute-start | bytes 43016 | tf_op jit(solution)/shard_map/ppermute | solution.py:23
  31.4 92.7 %copy-start.2 = (bf16[32,64,64]{2,1,0:T(8,128)(2,1)S(1)}, bf16[32,64,64]{2,1,0:T(8,128)(2,1)}, u32[]{:S(2)}) copy-start(bf16[32,64,64]{2,1,0:T(8,128)(2,1)} %param.35) | copy-start | bytes 786436
  31.4 93.7 %copy-start.8 = (s32[96,8]{0,1:T(8,128)S(1)}, s32[96,8]{0,1:T(8,128)}, u32[]{:S(2)}) copy-start(s32[96,8]{0,1:T(8,128)} %param.23) | copy-start | bytes 9220
  33.3 92.9 %copy-start.5 = (bf16[1,64,64]{2,1,0:T(8,128)(2,1)S(1)}, bf16[1,64,64]{2,1,0:T(8,128)(2,1)}, u32[]{:S(2)}) copy-start(bf16[1,64,64]{2,1,0:T(8,128)(2,1)} %param.36) | copy-start | bytes 24580
  46.3 107.6 %collective-permute-start.3 = (bf16[8,2048]{1,0:T(8,128)(2,1)S(1)}, bf16[8,2048]{1,0:T(8,128)(2,1)S(1)}, u32[]{:S(2)}, u32[]{:S(2)}) collective-permute-start(bf16[8,2048]{1,0:T(8,128)(2,1)S(1)} %bitcast.165), channel_id=1, source_target_pairs={{8,0},{16,8},{24,16},{32,24},{40,32},{48,40},{56,48},{64,56},{72,6... | collective-permute-start | bytes 98312 | tf_op jit(solution)/shard_map/ppermute | solution.py:23
  149.5 12.5 %collective-permute-start.2 = (bf16[8,2048]{1,0:T(8,128)(2,1)S(1)}, bf16[8,2048]{1,0:T(8,128)(2,1)S(1)}, u32[]{:S(2)}, u32[]{:S(2)}) collective-permute-start(bf16[8,2048]{1,0:T(8,128)(2,1)S(1)} %bitcast.166), channel_id=1, source_target_pairs={{0,8},{8,16},{16,24},{24,32},{32,40},{40,48},{48,56},{56,64},{64,7... | collective-permute-start | bytes 98312 | tf_op jit(solution)/shard_map/ppermute | solution.py:21
  152.0 11.5 %collective-permute-start.4 = (bf16[4,32,128]{2,1,0:T(8,128)(2,1)S(1)}, bf16[4,32,128]{2,1,0:T(8,128)(2,1)S(1)}, u32[]{:S(2)}, u32[]{:S(2)}) collective-permute-start(bf16[4,32,128]{2,1,0:T(8,128)(2,1)S(1)} %get-tuple-element.80), channel_id=1, source_target_pairs={{0,1},{1,2},{2,3},{3,4},{4,5},{5,6},{6,7},{7,8},{8,9},{9,10},{10,1... | collective-permute-start | bytes 98312 | tf_op jit(solution)/shard_map/ppermute | solution.py:21
  154.0 9.5 %collective-permute-start.5 = (bf16[4,32,128]{2,1,0:T(8,128)(2,1)S(1)}, bf16[4,32,128]{2,1,0:T(8,128)(2,1)S(1)}, u32[]{:S(2)}, u32[]{:S(2)}) collective-permute-start(bf16[4,32,128]{2,1,0:T(8,128)(2,1)S(1)} %get-tuple-element.81), channel_id=1, source_target_pairs={{1,0},{2,1},{3,2},{4,3},{5,4},{6,5},{7,6},{8,7},{9,8},{10,9},{11,1... | collective-permute-start | bytes 98312 | tf_op jit(solution)/shard_map/ppermute | solution.py:23
  306.1 11.7 %copy-start.1 = (f32[32,96,64]{2,0,1:T(8,128)S(1)}, f32[32,96,64]{2,0,1:T(8,128)}, u32[]{:S(2)}) copy-start(f32[32,96,64]{2,0,1:T(8,128)} %fusion.37) | copy-start | bytes 2359300
  306.1 11.7 %copy-start.3 = (bf16[96,6]{1,0:T(8,128)(2,1)S(1)}, bf16[96,6]{1,0:T(8,128)(2,1)}, u32[]{:S(2)}) copy-start(bf16[96,6]{1,0:T(8,128)(2,1)} %fusion.49) | copy-start | bytes 3460
  306.1 11.7 %copy-start.6 = (pred[96,6]{1,0:T(8,128)(4,1)S(1)}, pred[96,6]{1,0:T(8,128)(4,1)}, u32[]{:S(2)}) copy-start(pred[96,6]{1,0:T(8,128)(4,1)} %copy.64) | copy-start | bytes 1732
where the time goes:
time: 331 us; the launch traced here: 328 us
  matrix products  94.2 us (28%)
  local copies, waits for them, and re-layouts  90.2 us (27%)
  blocking collectives  85.2 us (26%)
  starting transfers between devices  35.4 us (11%)
  other arithmetic  22.2 us (7%)
    dot_general x12, matrix products, near_block(): jnp.einsum('bmnj,bnrj->brm', kernel, values, preferred_element_type=wide)  70.5 us
    all_gather x1, blocking collectives, on_device(): lax.all_gather(group_sum.astype(narrow), 'gx', axis=0, tiled=True)  48 us
    ppermute x4, starting transfers between devices, padded(): lax.ppermute(head, axis, [((i + 1) % count, i) for i in range(ends)])  27.2 us
    unnamed x30, local copies, waits for them, and re-layouts  25.5 us
    psum x1, blocking collectives, on_device(): group_sum = lax.psum(mid_term, 'gy')  24.5 us
    gather x2, local copies, waits for them, and re-layouts, on_device(): jnp.take(coeff_rim, leaf_far - (first_leaf - leaves), axis=0)  15.6 us
    all_gather x1, blocking collectives, on_device(): siblings = lax.all_gather(mid_flat, 'gy', axis=0, tiled=True)  12.8 us
    dot_general x1, matrix products, on_device(): jnp.einsum('lkr,lkm->lrm', leaf_field, basis_out, preferred_element_type=...  10.3 us
  transfers between devices with their start and end apart: 8, of which 0 were waited for; matrix products, arithmetic and copies ran while one was open for 53% of the time, Pallas kernels for 0%

commit v1 on v0

--- a/solution.py
+++ b/solution.py
@@ -83,7 +83,11 @@
     mid_term = jnp.dot(cluster_up[0], mid_coeffs, preferred_element_type=wide).reshape(1, flat)
     mid_flat = mid_coeffs.reshape(1, flat)
     siblings = lax.all_gather(mid_flat, "gy", axis=0, tiled=True)
-    group_sum = lax.psum(mid_term, "gy")
+    group_sum = mid_term
+    for hop in (1, 2, 4):
+        group_sum = group_sum + lax.ppermute(
+            group_sum, "gy", [(dev, dev ^ hop) for dev in range(8)]
+        )
     nearby = padded(siblings, (("gx", 0),), group_size)
     mid_picked = jnp.take(nearby, cluster_far[0] - (gx_index - 1) * group_size, axis=0)
     top_coeffs = lax.all_gather(group_sum.astype(narrow), "gx", axis=0, tiled=True)

time: 331 us -> 312 us (0.943)
  blocking collectives: 85.2 us -> 61.2 us
  waiting for transfers between devices: 0.02 us -> 3.67 us
    psum x1 -> x0, blocking collectives: 24.5 us -> none  [on_device(): group_sum = lax.psum(mid_term, 'gy')]
    ppermute x4, starting transfers between devices: 27.2 us -> 21.4 us  [padded(): lax.ppermute(head, axis, [((i + 1) % count, i) for i in range(ends)])]
    ppermute x0 -> x3, waiting for transfers between devices: none -> 3.65 us  [on_device(): lax.ppermute(group_sum, 'gy', [(dev, dev ^ hop) for dev in range(8)])]
  transfers between devices with their start and end apart: 8 -> 11, of which waited for: 0 -> 1; matrix products, arithmetic and copies ran while one was open for 53% -> 57% of each run, Pallas kernels for 0% -> 0%
where the time goes in v1:
time: 312 us; the launch traced here: 306 us
  matrix products  94.2 us (30%)
  local copies, waits for them, and re-layouts  91 us (29%)
  blocking collectives  61.2 us (20%)
  starting transfers between devices  32.7 us (10%)
  other arithmetic  22.8 us (7%)
  waiting for transfers between devices  3.67 us (1%)
    dot_general x12, matrix products, near_block(): jnp.einsum('bmnj,bnrj->brm', kernel, values, preferred_element_type=wide)  70.5 us
    all_gather x1, blocking collectives, on_device(): lax.all_gather(group_sum.astype(narrow), 'gx', axis=0, tiled=True)  48.5 us
    unnamed x30, local copies, waits for them, and re-layouts  26.1 us
    ppermute x4, starting transfers between devices, padded(): lax.ppermute(head, axis, [((i + 1) % count, i) for i in range(ends)])  21.4 us
    gather x2, local copies, waits for them, and re-layouts, on_device(): jnp.take(coeff_rim, leaf_far - (first_leaf - leaves), axis=0)  15.7 us
    all_gather x1, blocking collectives, on_device(): siblings = lax.all_gather(mid_flat, 'gy', axis=0, tiled=True)  12.8 us
    dot_general x1, matrix products, on_device(): jnp.einsum('lkr,lkm->lrm', leaf_field, basis_out, preferred_element_type=...  10.3 us
    ppermute x4, starting transfers between devices, padded(): lax.ppermute(tail, axis, [(i, (i + 1) % count) for i in range(ends)])  9.52 us
  transfers between devices with their start and end apart: 11, of which 1 were waited for; matrix products, arithmetic and copies ran while one was open for 57% of the time, Pallas kernels for 0%

profile of v1, /device:TPU:8, one launch (start us, length us, event | category | flops | bytes accessed | tf_op | source)
XLA Modules:
  0.0 306.3 jit_solution(16798051930908409114)
XLA Ops:
  4.9 9.3 %collective-permute-start.1 = (bf16[96,2048]{1,0:T(8,128)(2,1)}, bf16[96,2048]{1,0:T(8,128)(2,1)}, u32[]{:S(2)}, u32[]{:S(2)}) collective-permute-start(bf16[96,2048]{1,0:T(8,128)(2,1)} %copy.66), channel_id=1, source_target_pairs={{1,0},{2,1},{3,2},{4,3},{5,4},{6,5},{7,6},{8,7},{9,8},{10,9},{11,1... | collective-permute-start | bytes 1179656 | tf_op jit(solution)/shard_map/ppermute | solution.py:23
  19.4 8.0 %collective-permute-start.10 = (f32[4,7,128]{2,1,0:T(8,128)S(1)}, f32[4,7,128]{2,1,0:T(8,128)S(1)}, u32[]{:S(2)}, u32[]{:S(2)}) collective-permute-start(f32[4,7,128]{2,1,0:T(8,128)S(1)} %get-tuple-element.83), channel_id=1, source_target_pairs={{1,0},{2,1},{3,2},{4,3},{5,4},{6,5},{7,6},{8,7},{9,8},{10,9},{11,1... | collective-permute-start | bytes 43016 | tf_op jit(solution)/shard_map/ppermute | solution.py:23
  27.4 4.0 %copy.72 = bf16[96,64,64]{2,1,0:T(8,128)(2,1)} copy(bf16[96,64,64]{0,2,1:T(8,128)(2,1)} %param.26) | data formatting | bytes 1572864 | tf_op args[5]
  37.9 12.8 %all-gather = bf16[8,1,2048]{2,1,0:T(2,128)(2,1)S(1)} all-gather(bf16[1,1,2048]{2,1,0:T(2,128)(2,1)S(1)} %reshape.240), channel_id=1, replica_groups=mesh['gx'=32,'gy'=8] {'gy'}, dimensions={0}, use_global_device_ids=true | all-gather | bytes 36864 | tf_op jit(solution)/shard_map/all_gather | solution.py:85
  50.7 4.0 %copy.78 = bf16[96,64,64]{2,1,0:T(8,128)(2,1)} copy(bf16[96,64,64]{0,2,1:T(8,128)(2,1)} %param.27) | data formatting | bytes 1572864 | tf_op args[6]
  54.7 16.2 %copy.71 = bf16[96,6,64,64]{3,2,1,0:T(8,128)(2,1)} copy(bf16[96,6,64,64]{0,3,2,1:T(8,128)(2,1)} %param.28) | data formatting | bytes 9437184 | tf_op args[7]
  83.9 48.5 %all-gather.1 = bf16[32,1,2048]{2,1,0:T(2,128)(2,1)S(1)} all-gather(bf16[1,1,2048]{2,1,0:T(2,128)(2,1)S(1)} %convert_bitcast_fusion), channel_id=1, replica_groups=mesh['gx'=32,'gy'=8] {'gx'}, dimensions={0}, use_global_device_ids=true | all-gather | bytes 135168 | tf_op jit(solution)/shard_map/all_gather | solution.py:93
  142.9 130.8 %while.10 = (s32[]{:T(128)}, f32[12,8,32,128]{3,2,1,0:T(8,128)}, s32[12,8,8]{2,1,0:T(8,128)}, bf16[104,32,128]{2,1,0:T(8,128)(2,1)S(1)}, f32[104,7,128]{2,1,0:T(...) while((s32[]{:T(128)}, f32[12,8,32,128]{3,2,1,0:T(8,128)}, s32[12,8,8]{2,1,0:T(8,128)}, ...), condition=%wide.region_2.3_spmd, body=%wide.region_1.2_spmd.sunk | while | flops 87352896 | bytes 3410213 | solution.py:137
  147.9 5.9 %fusion.84 = f32[12,8,32,128]{3,2,1,0:T(8,128)} fusion(f32[12,8,32,128]{3,2,1,0:T(8,128)} %get-tuple-element.149, s32[]{:T(128)S(6)} %copy.97, f32[8,8,128]{2,1,0:T(8,128)S(1)} %bitcast.158, f32[8,128]{1,0:T(8,128)} %get-tuple-element.132, f32[8,8,128]{2,1,0:T(8,128)S(1)} %bitcast.159, f32[8,8,128]{2,1,0:T(8,128)S(1)} %bitcast.160, ...), kind=kOutput, calls=%fused_computation.21.clone.1 | convolution fusion | flops 87293952 | bytes 897092 | tf_op jit(solution)/shard_map/while/body/eval_jaxpr/bmnj,bnrj->brm/dot_general | solution.py:135
  158.8 5.9 %fusion.84 = f32[12,8,32,128]{3,2,1,0:T(8,128)} fusion(f32[12,8,32,128]{3,2,1,0:T(8,128)} %get-tuple-element.149, s32[]{:T(128)S(6)} %copy.97, f32[8,8,128]{2,1,0:T(8,128)S(1)} %bitcast.158, f32[8,128]{1,0:T(8,128)} %get-tuple-element.132, f32[8,8,128]{2,1,0:T(8,128)S(1)} %bitcast.159, f32[8,8,128]{2,1,0:T(8,128)S(1)} %bitcast.160, ...), kind=kOutput, calls=%fused_computation.21.clone.1 | convolution fusion | flops 87293952 | bytes 897092 | tf_op jit(solution)/shard_map/while/body/eval_jaxpr/bmnj,bnrj->brm/dot_general | solution.py:135
  169.7 5.9 %fusion.84 = f32[12,8,32,128]{3,2,1,0:T(8,128)} fusion(f32[12,8,32,128]{3,2,1,0:T(8,128)} %get-tuple-element.149, s32[]{:T(128)S(6)} %copy.97, f32[8,8,128]{2,1,0:T(8,128)S(1)} %bitcast.158, f32[8,128]{1,0:T(8,128)} %get-tuple-element.132, f32[8,8,128]{2,1,0:T(8,128)S(1)} %bitcast.159, f32[8,8,128]{2,1,0:T(8,128)S(1)} %bitcast.160, ...), kind=kOutput, calls=%fused_computation.21.clone.1 | convolution fusion | flops 87293952 | bytes 897092 | tf_op jit(solution)/shard_map/while/body/eval_jaxpr/bmnj,bnrj->brm/dot_general | solution.py:135
  180.6 5.9 %fusion.84 = f32[12,8,32,128]{3,2,1,0:T(8,128)} fusion(f32[12,8,32,128]{3,2,1,0:T(8,128)} %get-tuple-element.149, s32[]{:T(128)S(6)} %copy.97, f32[8,8,128]{2,1,0:T(8,128)S(1)} %bitcast.158, f32[8,128]{1,0:T(8,128)} %get-tuple-element.132, f32[8,8,128]{2,1,0:T(8,128)S(1)} %bitcast.159, f32[8,8,128]{2,1,0:T(8,128)S(1)} %bitcast.160, ...), kind=kOutput, calls=%fused_computation.21.clone.1 | convolution fusion | flops 87293952 | bytes 897092 | tf_op jit(solution)/shard_map/while/body/eval_jaxpr/bmnj,bnrj->brm/dot_general | solution.py:135
  191.5 5.9 %fusion.84 = f32[12,8,32,128]{3,2,1,0:T(8,128)} fusion(f32[12,8,32,128]{3,2,1,0:T(8,128)} %get-tuple-element.149, s32[]{:T(128)S(6)} %copy.97, f32[8,8,128]{2,1,0:T(8,128)S(1)} %bitcast.158, f32[8,128]{1,0:T(8,128)} %get-tuple-element.132, f32[8,8,128]{2,1,0:T(8,128)S(1)} %bitcast.159, f32[8,8,128]{2,1,0:T(8,128)S(1)} %bitcast.160, ...), kind=kOutput, calls=%fused_computation.21.clone.1 | convolution fusion | flops 87293952 | bytes 897092 | tf_op jit(solution)/shard_map/while/body/eval_jaxpr/bmnj,bnrj->brm/dot_general | solution.py:135
  202.4 5.9 %fusion.84 = f32[12,8,32,128]{3,2,1,0:T(8,128)} fusion(f32[12,8,32,128]{3,2,1,0:T(8,128)} %get-tuple-element.149, s32[]{:T(128)S(6)} %copy.97, f32[8,8,128]{2,1,0:T(8,128)S(1)} %bitcast.158, f32[8,128]{1,0:T(8,128)} %get-tuple-element.132, f32[8,8,128]{2,1,0:T(8,128)S(1)} %bitcast.159, f32[8,8,128]{2,1,0:T(8,128)S(1)} %bitcast.160, ...), kind=kOutput, calls=%fused_computation.21.clone.1 | convolution fusion | flops 87293952 | bytes 897092 | tf_op jit(solution)/shard_map/while/body/eval_jaxpr/bmnj,bnrj->brm/dot_general | solution.py:135
  213.3 5.9 %fusion.84 = f32[12,8,32,128]{3,2,1,0:T(8,128)} fusion(f32[12,8,32,128]{3,2,1,0:T(8,128)} %get-tuple-element.149, s32[]{:T(128)S(6)} %copy.97, f32[8,8,128]{2,1,0:T(8,128)S(1)} %bitcast.158, f32[8,128]{1,0:T(8,128)} %get-tuple-element.132, f32[8,8,128]{2,1,0:T(8,128)S(1)} %bitcast.159, f32[8,8,128]{2,1,0:T(8,128)S(1)} %bitcast.160, ...), kind=kOutput, calls=%fused_computation.21.clone.1 | convolution fusion | flops 87293952 | bytes 897092 | tf_op jit(solution)/shard_map/while/body/eval_jaxpr/bmnj,bnrj->brm/dot_general | solution.py:135
  224.2 5.9 %fusion.84 = f32[12,8,32,128]{3,2,1,0:T(8,128)} fusion(f32[12,8,32,128]{3,2,1,0:T(8,128)} %get-tuple-element.149, s32[]{:T(128)S(6)} %copy.97, f32[8,8,128]{2,1,0:T(8,128)S(1)} %bitcast.158, f32[8,128]{1,0:T(8,128)} %get-tuple-element.132, f32[8,8,128]{2,1,0:T(8,128)S(1)} %bitcast.159, f32[8,8,128]{2,1,0:T(8,128)S(1)} %bitcast.160, ...), kind=kOutput, calls=%fused_computation.21.clone.1 | convolution fusion | flops 87293952 | bytes 897092 | tf_op jit(solution)/shard_map/while/body/eval_jaxpr/bmnj,bnrj->brm/dot_general | solution.py:135
  235.1 5.9 %fusion.84 = f32[12,8,32,128]{3,2,1,0:T(8,128)} fusion(f32[12,8,32,128]{3,2,1,0:T(8,128)} %get-tuple-element.149, s32[]{:T(128)S(6)} %copy.97, f32[8,8,128]{2,1,0:T(8,128)S(1)} %bitcast.158, f32[8,128]{1,0:T(8,128)} %get-tuple-element.132, f32[8,8,128]{2,1,0:T(8,128)S(1)} %bitcast.159, f32[8,8,128]{2,1,0:T(8,128)S(1)} %bitcast.160, ...), kind=kOutput, calls=%fused_computation.21.clone.1 | convolution fusion | flops 87293952 | bytes 897092 | tf_op jit(solution)/shard_map/while/body/eval_jaxpr/bmnj,bnrj->brm/dot_general | solution.py:135
  246.0 5.9 %fusion.84 = f32[12,8,32,128]{3,2,1,0:T(8,128)} fusion(f32[12,8,32,128]{3,2,1,0:T(8,128)} %get-tuple-element.149, s32[]{:T(128)S(6)} %copy.97, f32[8,8,128]{2,1,0:T(8,128)S(1)} %bitcast.158, f32[8,128]{1,0:T(8,128)} %get-tuple-element.132, f32[8,8,128]{2,1,0:T(8,128)S(1)} %bitcast.159, f32[8,8,128]{2,1,0:T(8,128)S(1)} %bitcast.160, ...), kind=kOutput, calls=%fused_computation.21.clone.1 | convolution fusion | flops 87293952 | bytes 897092 | tf_op jit(solution)/shard_map/while/body/eval_jaxpr/bmnj,bnrj->brm/dot_general | solution.py:135
  256.9 5.9 %fusion.84 = f32[12,8,32,128]{3,2,1,0:T(8,128)} fusion(f32[12,8,32,128]{3,2,1,0:T(8,128)} %get-tuple-element.149, s32[]{:T(128)S(6)} %copy.97, f32[8,8,128]{2,1,0:T(8,128)S(1)} %bitcast.158, f32[8,128]{1,0:T(8,128)} %get-tuple-element.132, f32[8,8,128]{2,1,0:T(8,128)S(1)} %bitcast.159, f32[8,8,128]{2,1,0:T(8,128)S(1)} %bitcast.160, ...), kind=kOutput, calls=%fused_computation.21.clone.1 | convolution fusion | flops 87293952 | bytes 897092 | tf_op jit(solution)/shard_map/while/body/eval_jaxpr/bmnj,bnrj->brm/dot_general | solution.py:135
  267.8 5.9 %fusion.84 = f32[12,8,32,128]{3,2,1,0:T(8,128)} fusion(f32[12,8,32,128]{3,2,1,0:T(8,128)} %get-tuple-element.149, s32[]{:T(128)S(6)} %copy.97, f32[8,8,128]{2,1,0:T(8,128)S(1)} %bitcast.158, f32[8,128]{1,0:T(8,128)} %get-tuple-element.132, f32[8,8,128]{2,1,0:T(8,128)S(1)} %bitcast.159, f32[8,8,128]{2,1,0:T(8,128)S(1)} %bitcast.160, ...), kind=kOutput, calls=%fused_computation.21.clone.1 | convolution fusion | flops 87293952 | bytes 897092 | tf_op jit(solution)/shard_map/while/body/eval_jaxpr/bmnj,bnrj->brm/dot_general | solution.py:135
  274.8 4.2 %fusion.37 = f32[32,96,64]{2,0,1:T(8,128)} fusion(bf16[96,64,64]{2,1,0:T(8,128)(2,1)} %copy.78, f32[32,64]{1,0:T(8,128)S(1)} %convolution_bitcast_fusion.3, bf16[32,64]{1,0:T(8,128)(2,1)} %fusion.33, bf16[1,64,64]{2,1,0:T(8,128)(2,1)} %param.32), kind=kOutput, calls=%fused_computation.60 | convolution fusion | flops 25432064 | bytes 1593344 | tf_op jit(solution)/shard_map/lik,kr->lir/dot_general | solution.py:123
  280.4 4.0 %gather_fusion.2 = bf16[576,2048]{1,0:T(8,128)(2,1)} fusion(bf16[288,2048]{1,0:T(8,128)(2,1)S(1)} %pad_maximum_fusion, s32[1024]{0:T(1024)S(1)} %pad_clamp_fusion.3), kind=kCustom, calls=%fused_computation.2 | custom fusion | bytes 4720896 | tf_op jit(solution)/shard_map/jit(_take)/gather | solution.py:114
  284.4 11.7 %gather.23 = bf16[96,6,64,32]{3,2,1,0:T(8,128)(2,1)} reshape(bf16[576,2048]{1,0:T(8,128)(2,1)} %gather_fusion.2) | data formatting | bytes 4718592 | tf_op jit(solution)/shard_map/jit(_take)/gather | solution.py:114
  296.1 10.3 %bitcast_add_fusion.1 = f32[96,32,128]{2,1,0:T(8,128)} fusion(f32[12,8,32,128]{3,2,1,0:T(8,128)} %get-tuple-element.37, bf16[96,64,128]{2,1,0:T(8,128)(2,1)S(1)} %copy-done, f32[32,96,64]{2,0,1:T(8,128)S(1)} %copy-done.1, bf16[96,6,64,64]{3,2,1,0:T(8,128)(2,1)} %copy.71, bf16[96,6,64,32]{3,2,1,0:T(8,128)(2,1)} %gather.23, pred[96,6]{1,0:T(8,128)(4,1)S(1)} %copy-done.6, ...), kind=kOutput, calls=%fused_computation.44 | convolution fusion | flops 204472320 | bytes 12584640 | tf_op jit(solution)/shard_map/lkr,lkm->lrm/dot_general | solution.py:125
  (209 shorter events, 102.2 us)
Async XLA Ops:
  0.0 296.1 %copy-start = (bf16[96,64,128]{2,1,0:T(8,128)(2,1)S(1)}, bf16[96,64,128]{2,1,0:T(8,128)(2,1)}, u32[]{:S(2)}) copy-start(bf16[96,64,128]{2,1,0:T(8,128)(2,1)} %param.25) | copy-start | bytes 4718596
  4.9 274.1 %collective-permute-start.1 = (bf16[96,2048]{1,0:T(8,128)(2,1)}, bf16[96,2048]{1,0:T(8,128)(2,1)}, u32[]{:S(2)}, u32[]{:S(2)}) collective-permute-start(bf16[96,2048]{1,0:T(8,128)(2,1)} %copy.66), channel_id=1, source_target_pairs={{1,0},{2,1},{3,2},{4,3},{5,4},{6,5},{7,6},{8,7},{9,8},{10,9},{11,1... | collective-permute-start | bytes 1179656 | tf_op jit(solution)/shard_map/ppermute | solution.py:23
  14.2 264.8 %collective-permute-start = (bf16[96,2048]{1,0:T(8,128)(2,1)}, bf16[96,2048]{1,0:T(8,128)(2,1)}, u32[]{:S(2)}, u32[]{:S(2)}) collective-permute-start(bf16[96,2048]{1,0:T(8,128)(2,1)} %copy.66), channel_id=1, source_target_pairs={{0,1},{1,2},{2,3},{3,4},{4,5},{5,6},{6,7},{7,8},{8,9},{9,10},{10,1... | collective-permute-start | bytes 1179656 | tf_op jit(solution)/shard_map/ppermute | solution.py:21
  17.4 55.6 %collective-permute-start.9 = (f32[4,7,128]{2,1,0:T(8,128)S(1)}, f32[4,7,128]{2,1,0:T(8,128)S(1)}, u32[]{:S(2)}, u32[]{:S(2)}) collective-permute-start(f32[4,7,128]{2,1,0:T(8,128)S(1)} %get-tuple-element.82), channel_id=1, source_target_pairs={{0,1},{1,2},{2,3},{3,4},{4,5},{5,6},{6,7},{7,8},{8,9},{9,10},{10,1... | collective-permute-start | bytes 43016 | tf_op jit(solution)/shard_map/ppermute | solution.py:21
  19.3 14.0 %copy-start.5 = (bf16[1,64,64]{2,1,0:T(8,128)(2,1)S(1)}, bf16[1,64,64]{2,1,0:T(8,128)(2,1)}, u32[]{:S(2)}) copy-start(bf16[1,64,64]{2,1,0:T(8,128)(2,1)} %param.31) | copy-start | bytes 24580
  19.3 14.4 %copy-start.10 = (s32[1,6]{1,0:T(1,128)S(1)}, s32[1,6]{1,0:T(1,128)}, u32[]{:S(2)}) copy-start(s32[1,6]{1,0:T(1,128)} %param.34) | copy-start | bytes 76
  19.3 14.5 %copy-start.11 = (s32[1,6]{1,0:T(1,128)S(1)}, s32[1,6]{1,0:T(1,128)}, u32[]{:S(2)}) copy-start(s32[1,6]{1,0:T(1,128)} %param.38) | copy-start | bytes 76
  19.3 15.8 %copy-start.9 = (s32[96]{0:T(128)S(1)}, s32[96]{0:T(128)}, u32[]{:S(2)}) copy-start(s32[96]{0:T(128)} %param.30) | copy-start | bytes 1156
  19.3 16.5 %copy-start.7 = (s32[96,6]{0,1:T(8,128)S(1)}, s32[96,6]{0,1:T(8,128)}, u32[]{:S(2)}) copy-start(s32[96,6]{0,1:T(8,128)} %param.29) | copy-start | bytes 6916
  19.3 16.7 %copy-start.8 = (s32[96,8]{0,1:T(8,128)S(1)}, s32[96,8]{0,1:T(8,128)}, u32[]{:S(2)}) copy-start(s32[96,8]{0,1:T(8,128)} %param.23) | copy-start | bytes 9220
  19.4 57.3 %collective-permute-start.10 = (f32[4,7,128]{2,1,0:T(8,128)S(1)}, f32[4,7,128]{2,1,0:T(8,128)S(1)}, u32[]{:S(2)}, u32[]{:S(2)}) collective-permute-start(f32[4,7,128]{2,1,0:T(8,128)S(1)} %get-tuple-element.83), channel_id=1, source_target_pairs={{1,0},{2,1},{3,2},{4,3},{5,4},{6,5},{7,6},{8,7},{9,8},{10,9},{11,1... | collective-permute-start | bytes 43016 | tf_op jit(solution)/shard_map/ppermute | solution.py:23
  33.6 4.1 %collective-permute-start.4 = (f32[1,2048]{1,0:T(1,128)S(1)}, f32[1,2048]{1,0:T(1,128)S(1)}, u32[]{:S(2)}, u32[]{:S(2)}) collective-permute-start(f32[1,2048]{1,0:T(1,128)S(1)} %reshape.189), channel_id=1, source_target_pairs={{0,1},{1,0},{2,3},{3,2},{4,5},{5,4},{6,7},{7,6},{8,9},{9,8},{10,11... | collective-permute-start | bytes 24584 | tf_op jit(solution)/shard_map/ppermute | solution.py:88
  37.8 33.0 %collective-permute-start.5 = (f32[1,2048]{1,0:T(1,128)S(1)}, f32[1,2048]{1,0:T(1,128)S(1)}, u32[]{:S(2)}, u32[]{:S(2)}) collective-permute-start(f32[1,2048]{1,0:T(1,128)S(1)} %add.124), channel_id=1, source_target_pairs={{0,2},{1,3},{2,0},{3,1},{4,6},{5,7},{6,4},{7,5},{8,10},{9,11},{10,... | collective-permute-start | bytes 24584 | tf_op jit(solution)/shard_map/ppermute | solution.py:88
  54.7 78.8 %copy-start.2 = (bf16[32,64,64]{2,1,0:T(8,128)(2,1)S(1)}, bf16[32,64,64]{2,1,0:T(8,128)(2,1)}, u32[]{:S(2)}) copy-start(bf16[32,64,64]{2,1,0:T(8,128)(2,1)} %param.35) | copy-start | bytes 786436
  70.8 66.7 %collective-permute-start.3 = (bf16[8,2048]{1,0:T(8,128)(2,1)S(1)}, bf16[8,2048]{1,0:T(8,128)(2,1)S(1)}, u32[]{:S(2)}, u32[]{:S(2)}) collective-permute-start(bf16[8,2048]{1,0:T(8,128)(2,1)S(1)} %bitcast.164), channel_id=1, source_target_pairs={{8,0},{16,8},{24,16},{32,24},{40,32},{48,40},{56,48},{64,56},{72,6... | collective-permute-start | bytes 98312 | tf_op jit(solution)/shard_map/ppermute | solution.py:23
  72.9 66.6 %collective-permute-start.2 = (bf16[8,2048]{1,0:T(8,128)(2,1)S(1)}, bf16[8,2048]{1,0:T(8,128)(2,1)S(1)}, u32[]{:S(2)}, u32[]{:S(2)}) collective-permute-start(bf16[8,2048]{1,0:T(8,128)(2,1)S(1)} %bitcast.165), channel_id=1, source_target_pairs={{0,8},{8,16},{16,24},{24,32},{32,40},{40,48},{48,56},{56,64},{64,7... | collective-permute-start | bytes 98312 | tf_op jit(solution)/shard_map/ppermute | solution.py:21
  76.7 5.2 %collective-permute-start.6 = (f32[1,2048]{1,0:T(1,128)S(1)}, f32[1,2048]{1,0:T(1,128)S(1)}, u32[]{:S(2)}, u32[]{:S(2)}) collective-permute-start(f32[1,2048]{1,0:T(1,128)S(1)} %add.125), channel_id=1, source_target_pairs={{0,4},{1,5},{2,6},{3,7},{4,0},{5,1},{6,2},{7,3},{8,12},{9,13},{10,... | collective-permute-start | bytes 24584 | tf_op jit(solution)/shard_map/ppermute | solution.py:88
  81.9 59.0 %collective-permute-start.7 = (bf16[4,32,128]{2,1,0:T(8,128)(2,1)S(1)}, bf16[4,32,128]{2,1,0:T(8,128)(2,1)S(1)}, u32[]{:S(2)}, u32[]{:S(2)}) collective-permute-start(bf16[4,32,128]{2,1,0:T(8,128)(2,1)S(1)} %get-tuple-element.80), channel_id=1, source_target_pairs={{0,1},{1,2},{2,3},{3,4},{4,5},{5,6},{6,7},{7,8},{8,9},{9,10},{10,1... | collective-permute-start | bytes 98312 | tf_op jit(solution)/shard_map/ppermute | solution.py:21
  137.5 4.1 %collective-permute-start.8 = (bf16[4,32,128]{2,1,0:T(8,128)(2,1)S(1)}, bf16[4,32,128]{2,1,0:T(8,128)(2,1)S(1)}, u32[]{:S(2)}, u32[]{:S(2)}) collective-permute-start(bf16[4,32,128]{2,1,0:T(8,128)(2,1)S(1)} %get-tuple-element.81), channel_id=1, source_target_pairs={{1,0},{2,1},{3,2},{4,3},{5,4},{6,5},{7,6},{8,7},{9,8},{10,9},{11,1... | collective-permute-start | bytes 98312 | tf_op jit(solution)/shard_map/ppermute | solution.py:23
  141.0 0.6 copy-start.3
  284.4 11.7 %copy-start.1 = (f32[32,96,64]{2,0,1:T(8,128)S(1)}, f32[32,96,64]{2,0,1:T(8,128)}, u32[]{:S(2)}) copy-start(f32[32,96,64]{2,0,1:T(8,128)} %fusion.37) | copy-start | bytes 2359300
  284.4 11.7 %copy-start.4 = (bf16[96,6]{1,0:T(8,128)(2,1)S(1)}, bf16[96,6]{1,0:T(8,128)(2,1)}, u32[]{:S(2)}) copy-start(bf16[96,6]{1,0:T(8,128)(2,1)} %fusion.49) | copy-start | bytes 3460
  284.4 11.7 %copy-start.6 = (pred[96,6]{1,0:T(8,128)(4,1)S(1)}, pred[96,6]{1,0:T(8,128)(4,1)}, u32[]{:S(2)}) copy-start(pred[96,6]{1,0:T(8,128)(4,1)} %copy.64) | copy-start | bytes 1732
